TPU v7x, 512 devices: a whole 4x8x8 slice. The times are simulated.
512 devices in a mesh: tile: 64 (over z, x, core), freq: 8 (over y).
Axes of the slice: x: 4, y: 8, z: 8, core: 2. Of those that a mesh axis runs over, the one named last changes fastest.
Arguments:
- u_factors: bfloat16 [8, 16384, 32, 128], P('freq', 'tile'), may hold values from -0.125 to 0.125
- v_factors: bfloat16 [8, 16384, 32, 128], P('freq', 'tile'), may hold values from -0.1875 to 0.1875
- ranks: int32 [8, 32, 32], P('freq'), may hold values from 8 to 64, as said below
- observed: float32 [8, 16384, 128], P('freq', 'tile'), may hold values from -6 to 6
- start: float32 [8, 16384, 128], P('freq', 'tile'), may hold values from -6 to 6
Outputs:
- estimate: float32 [8, 16384, 128], P('freq', 'tile')
Inputs may be any that keep to these rules, and one draw needn't show every extreme that they name: `ranks`: every frequency has a tile of rank 64 and a tile of rank 64 // 8.
All inputs are finite; a program needn't handle non-finite values.
Results may differ from a plain program's by a relative error of at most 0.0031.
Values may be sent and summed in bfloat16 or wider, within the bound.
A program may use at most 64 MiB of HBM per device.

v0:
```python
import math

import jax
import jax.numpy as jnp
from jax import lax
from jax.sharding import PartitionSpec as P

STEP_SIZE = 0.2
LEVEL = 0.5
TOP_PRECISION = lax.Precision.HIGHEST


def conj_product(blocks, rank_half, source_half):
    real_part = blocks[..., :rank_half, :source_half] + blocks[..., rank_half:, source_half:]
    imaginary = blocks[..., :rank_half, source_half:] - blocks[..., rank_half:, :source_half]
    return jnp.concatenate([real_part, imaginary], axis=-1)


def complex_stack(coeffs, source_half):
    lower_rows = jnp.concatenate([-coeffs[..., source_half:], coeffs[..., :source_half]], axis=-1)
    return jnp.concatenate([coeffs, lower_rows], axis=-2)


def band_tables(band_ids, band_size):
    phases = (
        2.0
        * jnp.pi
        * band_ids.astype(jnp.float32)[:, None]
        * jnp.arange(band_size, dtype=jnp.float32)[None, :]
        / band_size
    )
    return (jnp.cos(phases), jnp.sin(phases))


def to_time(spectra, cosine_matrix, sine_matrix):
    source_half = spectra.shape[-1] // 2
    factor = 1.0 / math.sqrt(cosine_matrix.shape[1])
    input_real = spectra[..., :source_half]
    imaginary_input = spectra[..., source_half:]
    output_real = jnp.einsum(
        "bg,biq->giq", cosine_matrix, input_real, precision=TOP_PRECISION
    ) - jnp.einsum("bg,biq->giq", sine_matrix, imaginary_input, precision=TOP_PRECISION)
    imaginary_output = jnp.einsum(
        "bg,biq->giq", sine_matrix, input_real, precision=TOP_PRECISION
    ) + jnp.einsum("bg,biq->giq", cosine_matrix, imaginary_input, precision=TOP_PRECISION)
    return jnp.concatenate([output_real, imaginary_output], axis=-1) * factor


def to_freq(samples, cosine_matrix, sine_matrix):
    source_half = samples.shape[-1] // 2
    factor = 1.0 / math.sqrt(cosine_matrix.shape[1])
    input_real = samples[..., :source_half]
    imaginary_input = samples[..., source_half:]
    output_real = jnp.einsum(
        "be,evi->bvi", cosine_matrix, input_real, precision=TOP_PRECISION
    ) + jnp.einsum("be,evi->bvi", sine_matrix, imaginary_input, precision=TOP_PRECISION)
    imaginary_output = jnp.einsum(
        "be,evi->bvi", cosine_matrix, imaginary_input, precision=TOP_PRECISION
    ) - jnp.einsum("be,evi->bvi", sine_matrix, input_real, precision=TOP_PRECISION)
    return jnp.concatenate([output_real, imaginary_output], axis=-1) * factor


def thin_out(values):
    return values - jnp.clip(values, -LEVEL, LEVEL)


def body(u_factors, v_factors, ranks, observed, start):
    local_freqs = v_factors.shape[0]
    tile_rows = v_factors.shape[2]
    rank_max = v_factors.shape[3] // 2
    tile_cols = u_factors.shape[2]
    source_half = start.shape[2] // 2
    tile_count = lax.axis_size("tile")
    group_size = tile_count // tile_rows
    position = lax.axis_index("tile")
    column = position // 2
    owner_row = position // group_size
    rank_ids = jnp.arange(rank_max, dtype=jnp.int32)
    column_ranks = lax.dynamic_slice_in_dim(ranks, column, 1, 2)[:, :, 0]
    column_mask = (rank_ids[None, None, :] < column_ranks[:, :, None]).astype(jnp.float32)[
        ..., None
    ]
    row_ranks = lax.dynamic_slice_in_dim(ranks, owner_row, 1, 1)[:, 0, :]
    row_mask = (rank_ids[None, None, :] < row_ranks[:, :, None]).astype(jnp.float32)[..., None]
    band_size = lax.axis_size("freq") * local_freqs
    estimate = start
    estimate_low = estimate.astype(jnp.bfloat16)
    blocks = jnp.einsum(
        "fcik,fcs->fiks", v_factors, estimate_low, preferred_element_type=jnp.float32
    )
    partial_value = conj_product(blocks, rank_max, source_half).astype(jnp.bfloat16)
    outgoing = jnp.repeat(partial_value, group_size, axis=1)
    arrived = lax.all_to_all(outgoing, "tile", split_axis=1, concat_axis=1, tiled=True)
    paired_sum = (
        arrived.astype(jnp.float32)
        .reshape(local_freqs, tile_cols, 2, rank_max, 2 * source_half)
        .sum(axis=2)
    )
    coeffs = (paired_sum * row_mask).astype(jnp.bfloat16)
    image_rows = jnp.einsum(
        "frjk,fjks->frs",
        u_factors,
        complex_stack(coeffs, source_half),
        preferred_element_type=jnp.float32,
    )
    misfit = image_rows - observed
    back_blocks = jnp.einsum(
        "frjk,frs->fjks", u_factors, misfit.astype(jnp.bfloat16), preferred_element_type=jnp.float32
    )
    back_part = conj_product(back_blocks, rank_max, source_half).astype(jnp.bfloat16)
    outgoing = jnp.repeat(back_part, 2, axis=1)
    arrived = lax.all_to_all(outgoing, "tile", split_axis=1, concat_axis=1, tiled=True)
    group_sum = (
        arrived.astype(jnp.float32)
        .reshape(local_freqs, tile_rows, group_size, rank_max, 2 * source_half)
        .sum(axis=2)
    )
    back_coeffs = (group_sum * column_mask).astype(jnp.bfloat16)
    gradient = jnp.einsum(
        "fcik,fiks->fcs",
        v_factors,
        complex_stack(back_coeffs, source_half),
        preferred_element_type=jnp.float32,
    )
    estimate = estimate - STEP_SIZE * gradient
    columns = lax.all_to_all(estimate, "freq", split_axis=1, concat_axis=0, tiled=True)
    cosine_matrix, sine_matrix = band_tables(jnp.arange(band_size, dtype=jnp.int32), band_size)
    thinned = thin_out(to_time(columns, cosine_matrix, sine_matrix))
    estimate = lax.all_to_all(
        to_freq(thinned, cosine_matrix, sine_matrix),
        "freq",
        split_axis=0,
        concat_axis=1,
        tiled=True,
    )
    return estimate


def solution(mesh):
    in_specs = (
        P("freq", "tile", None, None),
        P("freq", "tile", None, None),
        P("freq", None, None),
        P("freq", "tile", None),
        P("freq", "tile", None),
    )
    out_specs = P("freq", "tile", None)
    return jax.shard_map(body, mesh=mesh, in_specs=in_specs, out_specs=out_specs, check_vma=False)
```

profile of v0, /device:TPU:1, one launch (start us, length us, event | category | flops | bytes accessed | tf_op | source)
XLA Modules:
  0.0 125.5 jit_solution(4374031726351243664)
XLA Ops:
  0.0 3.3 %fusion.6 = f32[1,32,128,128]{3,2,1,0:T(8,128)S(1)} fusion(bf16[256,32,128]{2,1,0:T(8,128)(2,1)} %bitcast.109, f32[1,256,128]{2,1,0:T(8,128)} %param.9), kind=kOutput, calls=%fused_computation.10 | convolution fusion | flops 268468224 | bytes 4325376 | tf_op jit(solution)/shard_map/fcik,fcs->fiks/dot_general | solution.py:88
  3.3 0.6 fusion.37
  4.2 1.3 %broadcast_in_dim.16 = bf16[32,2,64,128]{3,2,1,0:T(8,128)(2,1)} broadcast(bf16[32,64,128]{2,1,0:T(8,128)(2,1)S(1)} %pad_maximum_fusion), dimensions={0,2,3} | broadcast | bytes 1572864 | tf_op jit(solution)/shard_map/broadcast_in_dim | solution.py:92
  5.5 14.8 %all-to-all-start = ((bf16[1,64,64,128]{3,2,0,1:T(8,128)(2,1)}), bf16[1,64,64,128]{3,2,0,1:T(8,128)(2,1)S(1)}, u32[]{:S(2)}, u32[]{:S(2)}) async-start(bf16[1,64,64,128]{3,2,0,1:T(8,128)(2,1)} %bitcast.8), calls=%async_computation | async-start | bytes 2097152 | tf_op jit(solution)/shard_map/all_to_all | solution.py:93
  20.4 2.7 %copy.54 = bf16[256,32,128]{0,2,1:T(8,128)(2,1)} copy(bf16[256,32,128]{2,1,0:T(8,128)(2,1)S(1)} %bitcast.108) | data formatting | bytes 4194304 | tf_op jit(solution)/shard_map/reshape.11
  23.3 25.2 %all-to-all-done = bf16[1,64,64,128]{3,2,0,1:T(8,128)(2,1)S(1)} async-done(((bf16[1,64,64,128]{3,2,0,1:T(8,128)(2,1)}), bf16[1,64,64,128]{3,2,0,1:T(8,128)(2,1)S(1)}, u32[]{:S(2)}, u32[]{:S(2)}) %all-to-all-start) | async-done | bytes 1048608 | tf_op jit(solution)/shard_map/all_to_all | solution.py:93
  48.7 0.6 copy.50
  49.6 1.1 slice_negate_fusion.1
  50.7 4.2 %fusion.36 = f32[128,4096]{0,1:S(1)} fusion(bf16[256,4096]{0,1:T(8,128)(2,1)} %bitcast.105, f32[1,256,128]{1,2,0:T(8,128)S(1)} %copy.52, bf16[256,32,128]{0,2,1:T(8,128)(2,1)} %copy.54, bf16[1,32,64,64]{2,3,1,0:T(8,128)(2,1)} %get-tuple-element.12, bf16[1,32,64,64]{2,3,1,0:T(8,128)(2,1)} %get-tuple-element.11, bf16[1,32,64,128]{2,3,1,0:T(8,128)(2,1)S(1)} %fusion.1), kind=kOutput, calls=%fused_computation.41 | convolution fusion | flops 540082176 | bytes 7471104
  54.9 0.6 fusion.39
  55.9 1.3 %broadcast_in_dim.18 = bf16[32,2,64,128]{3,2,1,0:T(8,128)(2,1)} broadcast(bf16[32,64,128]{2,1,0:T(8,128)(2,1)S(1)} %pad_maximum_fusion.1), dimensions={0,2,3} | broadcast | bytes 1572864 | tf_op jit(solution)/shard_map/broadcast_in_dim | solution.py:111
  57.2 6.3 %all-to-all-start.1 = ((bf16[1,64,64,128]{3,2,0,1:T(8,128)(2,1)}), bf16[1,64,64,128]{3,2,0,1:T(8,128)(2,1)S(1)}, u32[]{:S(2)}, u32[]{:S(2)}) async-start(bf16[1,64,64,128]{3,2,0,1:T(8,128)(2,1)} %bitcast.26), calls=%async_computation.1 | async-start | bytes 2097152 | tf_op jit(solution)/shard_map/all_to_all | solution.py:112
  63.8 27.8 %all-to-all-done.1 = bf16[1,64,64,128]{3,2,0,1:T(8,128)(2,1)S(1)} async-done(((bf16[1,64,64,128]{3,2,0,1:T(8,128)(2,1)}), bf16[1,64,64,128]{3,2,0,1:T(8,128)(2,1)S(1)}, u32[]{:S(2)}, u32[]{:S(2)}) %all-to-all-start.1) | async-done | bytes 1048608 | tf_op jit(solution)/shard_map/all_to_all | solution.py:112
  91.8 0.6 copy.55
  92.8 1.2 copy-done.2
  94.0 1.1 fusion.19
  95.2 0.8 copy.58
  95.9 6.8 %all-to-all-start.2 = ((f32[1,256,128]{2,0,1:T(1,128)}), f32[1,256,128]{2,0,1:T(1,128)S(1)}, u32[]{:S(2)}, u32[]{:S(2)}) async-start(f32[1,256,128]{2,0,1:T(1,128)} %copy.58), calls=%async_computation.2 | async-start | bytes 262144 | tf_op jit(solution)/shard_map/all_to_all | solution.py:126
  102.8 8.0 %all-to-all-done.2 = f32[1,256,128]{2,0,1:T(1,128)S(1)} async-done(((f32[1,256,128]{2,0,1:T(1,128)}), f32[1,256,128]{2,0,1:T(1,128)S(1)}, u32[]{:S(2)}, u32[]{:S(2)}) %all-to-all-start.2) | async-done | bytes 131104 | tf_op jit(solution)/shard_map/all_to_all | solution.py:126
  110.9 0.4 fusion.51
  111.3 0.4 fusion.49
  111.8 0.4 convolution_subtract_fusion.1
  114.4 10.4 %all_to_all.34 = f32[8,32,128]{2,1,0:T(8,128)S(1)} all-to-all(f32[8,32,128]{2,1,0:T(8,128)S(1)} %copy.65), channel_id=1, replica_groups=mesh['tile'=64,'freq'=8] {'freq'}, dimensions={0} | all-to-all | bytes 262144 | tf_op jit(solution)/shard_map/all_to_all | solution.py:129
  124.8 0.7 copy.100
  (32 shorter events, 4.4 us)
Async XLA Ops:
  0.0 23.2 %copy-start = (s32[1,32,32]{2,1,0:T(8,128)S(1)}, s32[1,32,32]{2,1,0:T(8,128)}, u32[]{:S(2)}) copy-start(s32[1,32,32]{2,1,0:T(8,128)} %param.7) | copy-start | bytes 12292
  4.2 16.2 %copy-start.1 = (bf16[1,256,32,128]{3,2,1,0:T(8,128)(2,1)S(1)}, bf16[1,256,32,128]{3,2,1,0:T(8,128)(2,1)}, u32[]{:S(2)}) copy-start(bf16[1,256,32,128]{3,2,1,0:T(8,128)(2,1)} %param.5) | copy-start | bytes 6291460
  5.5 43.0 %all-to-all-start = ((bf16[1,64,64,128]{3,2,0,1:T(8,128)(2,1)}), bf16[1,64,64,128]{3,2,0,1:T(8,128)(2,1)S(1)}, u32[]{:S(2)}, u32[]{:S(2)}) async-start(bf16[1,64,64,128]{3,2,0,1:T(8,128)(2,1)} %bitcast.8), calls=%async_computation | async-start | bytes 2097152 | tf_op jit(solution)/shard_map/all_to_all | solution.py:93
  20.4 2.7 %copy-start.4 = (f32[1,256,128]{2,1,0:T(8,128)S(1)}, f32[1,256,128]{2,1,0:T(8,128)}, u32[]{:S(2)}) copy-start(f32[1,256,128]{2,1,0:T(8,128)} %param.8) | copy-start | bytes 393220
  55.9 7.6 %copy-start.3 = (f32[1,256,128]{2,1,0:T(8,128)S(1)}, f32[1,256,128]{2,1,0:T(8,128)}, u32[]{:S(2)}) copy-start(f32[1,256,128]{2,1,0:T(8,128)} %param.9) | copy-start | bytes 393220
  57.2 34.4 %all-to-all-start.1 = ((bf16[1,64,64,128]{3,2,0,1:T(8,128)(2,1)}), bf16[1,64,64,128]{3,2,0,1:T(8,128)(2,1)S(1)}, u32[]{:S(2)}, u32[]{:S(2)}) async-start(bf16[1,64,64,128]{3,2,0,1:T(8,128)(2,1)} %bitcast.26), calls=%async_computation.1 | async-start | bytes 2097152 | tf_op jit(solution)/shard_map/all_to_all | solution.py:112
  92.4 1.6 %copy-start.2 = (bf16[1,256,32,128]{3,2,1,0:T(8,128)(2,1)S(1)}, bf16[1,256,32,128]{3,2,1,0:T(8,128)(2,1)}, u32[]{:S(2)}) copy-start(bf16[1,256,32,128]{3,2,1,0:T(8,128)(2,1)} %param.6) | copy-start | bytes 6291460
  95.9 14.9 %all-to-all-start.2 = ((f32[1,256,128]{2,0,1:T(1,128)}), f32[1,256,128]{2,0,1:T(1,128)S(1)}, u32[]{:S(2)}, u32[]{:S(2)}) async-start(f32[1,256,128]{2,0,1:T(1,128)} %copy.58), calls=%async_computation.2 | async-start | bytes 262144 | tf_op jit(solution)/shard_map/all_to_all | solution.py:126
where the time goes:
time: 128 us; the launch traced here: 125 us
  waiting for transfers between devices  61 us (48%)
  starting transfers between devices  27.9 us (22%)
  matrix products  11.8 us (9%)
  blocking collectives  10.4 us (8%)
  local copies, waits for them, and re-layouts  9.65 us (8%)
  other arithmetic  4.36 us (3%)
    all_to_all x2, waiting for transfers between devices, body(): lax.all_to_all(outgoing, 'tile', split_axis=1, concat_axis=1, tiled=True)  53 us
    all_to_all x2, starting transfers between devices, body(): lax.all_to_all(outgoing, 'tile', split_axis=1, concat_axis=1, tiled=True)  21.1 us
    all_to_all x1, blocking collectives, body(): lax.all_to_all(to_freq(thinned, cosine_matrix, sine_matrix), 'freq', spli...  10.4 us
    all_to_all x1, waiting for transfers between devices, body(): lax.all_to_all(estimate, 'freq', split_axis=1, concat_axis=0, tiled=True)  8.02 us
    all_to_all x1, starting transfers between devices, body(): lax.all_to_all(estimate, 'freq', split_axis=1, concat_axis=0, tiled=True)  6.82 us
    unnamed x1, matrix products  4.21 us
    dot_general x1, matrix products, body(): jnp.einsum('fcik,fcs->fiks', v_factors, estimate_low, preferred_element_t...  3.26 us
    another operation x1, local copies, waits for them, and re-layouts  2.73 us
  transfers between devices with their start and end apart: 3, of which 3 were waited for; matrix products, arithmetic and copies ran while one was open for 3% of the time, Pallas kernels for 0%

commit v1 on v0

v1 whole, which is shorter than its diff:
```python
import math

import jax
import jax.numpy as jnp
from jax import lax
from jax.experimental import pallas as pl
from jax.experimental.pallas import tpu as pltpu
from jax.sharding import PartitionSpec as P

STEP_SIZE = 0.2
LEVEL = 0.5
PLANE = (8, 4)
BANDS = 8
MESH = pl.DeviceIdType.MESH
BF16 = jnp.bfloat16
F32 = jnp.float32


def far_first(extent):
    order = sorted(range(extent), key=lambda d: (-min(d, extent - d), d))
    return order


def twiddle_pair(real, imag, cosine, sine):
    if abs(sine) < 1e-9:
        return (real, imag) if cosine > 0 else (-real, -imag)
    if abs(cosine) < 1e-9:
        return (-imag, real) if sine > 0 else (imag, -real)
    return real * cosine - imag * sine, real * sine + imag * cosine


def small_dft(reals, imags, sign):
    count = len(reals)
    if count == 1:
        return reals, imags
    even_re, even_im = small_dft(reals[0::2], imags[0::2], sign)
    odd_re, odd_im = small_dft(reals[1::2], imags[1::2], sign)
    out_re, out_im = [None] * count, [None] * count
    half = count // 2
    for k in range(half):
        angle = sign * 2.0 * math.pi * k / count
        tr, ti = twiddle_pair(odd_re[k], odd_im[k], math.cos(angle), math.sin(angle))
        out_re[k], out_im[k] = even_re[k] + tr, even_im[k] + ti
        out_re[k + half], out_im[k + half] = even_re[k] - tr, even_im[k] - ti
    return out_re, out_im


def thin_out(values):
    return values - jnp.clip(values, -LEVEL, LEVEL)


def kernel(
    ranks_ref, u_hbm, v_hbm, observed_hbm, start_hbm, out_ref,
    u_raw, v_raw, u_tiles, v_tiles, observed_rows, start_rows, start_t,
    pair_out, pair_own, pair_in, chip_out, chip_in, share_in,
    band_out, band_in, thin_out_buf, thin_in,
    load_sem, pair_send, pair_recv, chip_send, chip_recv, share_send, share_recv,
    band_send, band_recv,
):
    zc, xc = PLANE
    group = xc // 2
    bands = BANDS
    rows = u_raw.shape[0]
    lanes = u_raw.shape[2]
    rank_half = lanes // 2
    sources2 = start_t.shape[0]
    sources = sources2 // 2
    per_band = sources // bands

    place = lax.axis_index("tile")
    band = lax.axis_index("freq")
    chip = lax.div(place, 2)
    core = lax.rem(place, 2)
    other = 1 - core
    z = lax.div(chip, xc)
    x = lax.rem(chip, xc)
    order = far_first(zc)

    def shift_of(m, h, owner):
        return 2 * h + lax.rem(owner + order[m], 2)

    def chip_at(m, h, owner, forward):
        dz, dx = order[m], shift_of(m, h, owner)
        if forward:
            return lax.rem(z + dz, zc) * xc + lax.rem(x + dx, xc)
        return lax.rem(z + zc - dz, zc) * xc + lax.rem(x + xc - dx, xc)

    def is_self(m, h):
        return order[m] == 0 and h == 0

    def at_tile(index):
        return {"tile": index}

    barrier = pltpu.get_barrier_semaphore()

    def hail(device):
        pl.semaphore_signal(barrier, inc=1, device_id=device, device_id_type=MESH)

    for m in range(zc):
        for h in range(group):
            target = chip_at(m, h, core, True) * 2 + core
            if is_self(m, h):
                pl.when(core == 1)(lambda target=target: hail(at_tile(target)))
            else:
                hail(at_tile(target))
    hail(at_tile(chip * 2 + other))
    for k in range(1, bands):
        hail({"freq": lax.rem(band + k, bands)})

    loads = [
        pltpu.make_async_copy(start_hbm, start_rows, load_sem.at[0]),
        pltpu.make_async_copy(v_hbm, v_raw, load_sem.at[1]),
        pltpu.make_async_copy(observed_hbm, observed_rows, load_sem.at[2]),
        pltpu.make_async_copy(u_hbm, u_raw, load_sem.at[3]),
    ]
    for load in loads:
        load.start()

    def retile(raw, tiles):
        def step(b, carry):
            at = pl.multiple_of(b * 16, 16)
            tiles[:, pl.ds(at, 16), :] = jnp.swapaxes(raw[pl.ds(at, 16)], 0, 1)
            return carry
        lax.fori_loop(0, rows // 16, step, 0)

    lane_ids = lax.broadcasted_iota(jnp.int32, (sources, lanes), 1)
    upper = lane_ids < rank_half
    rank_ids = jnp.where(upper, lane_ids, lane_ids - rank_half)
    sign = jnp.where(upper, 1.0, -1.0).astype(F32)

    def swap_halves(values):
        return jnp.concatenate([values[:, rank_half:], values[:, :rank_half]], axis=1)

    def tile_group(tiles, m, owner, forward):
        return jnp.concatenate(
            [tiles[chip_at(m, h, owner, forward)] for h in range(group)], axis=1
        )

    def pair_copy(p, m):
        return pltpu.make_async_remote_copy(
            src_ref=pair_out.at[p, m], dst_ref=pair_in.at[p, m],
            send_sem=pair_send.at[p, m], recv_sem=pair_recv.at[p, m],
            device_id=at_tile(chip * 2 + other), device_id_type=MESH,
        )

    def chip_copy(p, m, h):
        return pltpu.make_async_remote_copy(
            src_ref=chip_out.at[p, m, h], dst_ref=chip_in.at[p, m, h],
            send_sem=chip_send.at[p, m, h], recv_sem=chip_recv.at[p, m, h],
            device_id=at_tile(chip_at(m, h, core, True) * 2 + core), device_id_type=MESH,
        )

    def share_copy(p, m):
        return pltpu.make_async_remote_copy(
            src_ref=chip_in.at[p, m], dst_ref=share_in.at[p, m],
            send_sem=share_send.at[p, m], recv_sem=share_recv.at[p, m],
            device_id=at_tile(chip * 2 + other), device_id_type=MESH,
        )

    def remote_only(m, h, act):
        if is_self(m, h):
            pl.when(core == 1)(act)
        else:
            act()

    def project(left, tiles, m, owner):
        product = jnp.dot(
            left, tile_group(tiles, m, owner, True), preferred_element_type=F32
        )
        parts = []
        for h in range(group):
            block = product[:, h * lanes : (h + 1) * lanes]
            parts.append(
                (block[:sources] * sign + swap_halves(block[sources:])).astype(BF16)
            )
        return parts

    def scatter(p, left, tiles, rank_of, ready):
        def give(m):
            for h, part in enumerate(project(left, tiles, m, other)):
                pair_out[p, m, h] = part
            if ready is None or m > 0:
                pair_copy(p, m).start()

        def keep(m):
            for h, part in enumerate(project(left, tiles, m, core)):
                pair_own[p, m, h] = part

        def finish(m):
            pair_copy(p, m).wait_recv()
            for h in range(group):
                total = pair_own[p, m, h].astype(F32) + pair_in[p, m, h].astype(F32)
                rank = rank_of(chip_at(m, h, core, True))
                total = jnp.where(rank_ids < rank, total, 0.0).astype(BF16)
                if is_self(m, h):
                    @pl.when(core == 0)
                    def _(total=total, m=m, h=h):
                        chip_in[p, m, h] = total

                def send(total=total, m=m, h=h):
                    chip_out[p, m, h] = total
                    chip_copy(p, m, h).start()

                remote_only(m, h, send)

        give(0)
        if ready is not None:
            ready()
            pair_copy(p, 0).start()
        for m in range(zc):
            if m + 1 < zc:
                give(m + 1)
            keep(m)
            finish(m)

    def stacked(coeffs):
        wide = coeffs.astype(F32)
        return jnp.concatenate([wide * sign, swap_halves(wide)], axis=0).astype(BF16)

    def expand(block, tiles, m, owner):
        left = jnp.concatenate([stacked(block[h]) for h in range(group)], axis=1)
        right = tile_group(tiles, m, owner, False)
        return lax.dot_general(
            left, right, (((1,), (1,)), ((), ())), preferred_element_type=F32
        )

    def collect(p, tiles):
        total = None
        for m in range(zc + 1):
            if m < zc:
                for h in range(group):
                    remote_only(m, h, lambda m=m, h=h: chip_copy(p, m, h).wait_recv())
                share_copy(p, m).start()
                term = expand(chip_in[p, m], tiles, m, core)
                total = term if total is None else total + term
            if m > 0:
                share_copy(p, m - 1).wait_recv()
                total = total + expand(share_in[p, m - 1], tiles, m - 1, other)
        return total

    loads[0].wait()
    start_t[...] = jnp.transpose(start_rows[...])
    loads[1].wait()
    retile(v_raw, v_tiles)

    scatter(
        0, start_t[...].astype(BF16), v_tiles,
        lambda target: ranks_ref[target, chip],
        lambda: pl.semaphore_wait(barrier, zc * group + bands - 1 + core),
    )
    loads[3].wait()
    retile(u_raw, u_tiles)
    loads[2].wait()
    observed_t = jnp.transpose(observed_rows[...])
    misfit = collect(0, u_tiles) - observed_t
    scatter(
        1, misfit.astype(BF16), u_tiles,
        lambda target: ranks_ref[chip, target],
        None,
    )
    estimate = start_t[...] - STEP_SIZE * collect(1, v_tiles)

    def band_copy(p, k):
        target = lax.rem(band + k, bands)
        src, dst = ((band_out, band_in), (thin_out_buf, thin_in))[p]
        return pltpu.make_async_remote_copy(
            src_ref=src.at[target], dst_ref=dst.at[band],
            send_sem=band_send.at[p, k], recv_sem=band_recv.at[p, k],
            device_id={"freq": target}, device_id_type=MESH,
        )

    def band_arrival(p, k):
        source = lax.rem(band + bands - k, bands)
        src, dst = ((band_out, band_in), (thin_out_buf, thin_in))[p]
        return pltpu.make_async_remote_copy(
            src_ref=src.at[source], dst_ref=dst.at[source],
            send_sem=band_send.at[p, k], recv_sem=band_recv.at[p, k],
            device_id={"freq": source}, device_id_type=MESH,
        )

    band_order = [k for k in far_first(bands) if k > 0]
    for q in range(bands):
        low = q * per_band
        slab = jnp.concatenate(
            [estimate[low : low + per_band], estimate[sources + low : sources + low + per_band]],
            axis=0,
        )
        band_out[q] = slab.astype(band_out.dtype)
    for k in band_order:
        band_copy(0, k).start()
    band_in[band] = band_out[band]
    for k in band_order:
        band_arrival(0, k).wait_recv()

    scale = 1.0 / math.sqrt(bands)
    slabs = [band_in[f].astype(F32) for f in range(bands)]
    reals = [slab[:per_band] for slab in slabs]
    imags = [slab[per_band:] for slab in slabs]
    reals, imags = small_dft(reals, imags, 1.0)
    reals = [thin_out(value * scale) for value in reals]
    imags = [thin_out(value * scale) for value in imags]
    reals, imags = small_dft(reals, imags, -1.0)
    for f in range(bands):
        slab = jnp.concatenate([reals[f], imags[f]], axis=0) * scale
        thin_out_buf[f] = slab.astype(thin_out_buf.dtype)
    for k in band_order:
        band_copy(1, k).start()
    thin_in[band] = thin_out_buf[band]
    for k in band_order:
        band_arrival(1, k).wait_recv()
    for q in range(bands):
        slab = thin_in[q].astype(F32)
        low = q * per_band
        out_ref[low : low + per_band, :] = slab[:per_band]
        out_ref[sources + low : sources + low + per_band, :] = slab[per_band:]

    for p in range(2):
        for m in range(zc):
            pair_copy(p, m).wait_send()
            share_copy(p, m).wait_send()
            for h in range(group):
                remote_only(m, h, lambda m=m, h=h: chip_copy(p, m, h).wait_send())
        for k in band_order:
            band_copy(p, k).wait_send()


def body(u_factors, v_factors, ranks, observed, start):
    zc, xc = PLANE
    bands = BANDS
    _, rows, tiles, lanes = u_factors.shape
    width = start.shape[2]
    group = xc // 2
    sources = width // 2
    per_band = sources // bands
    any_spec = pl.BlockSpec(memory_space=pl.ANY)
    block = (2, zc, group, sources, lanes)
    band_block = (bands, 2 * per_band, rows)
    result = pl.pallas_call(
        kernel,
        out_shape=jax.ShapeDtypeStruct((width, rows), F32),
        in_specs=[pl.BlockSpec(memory_space=pltpu.SMEM)] + [any_spec] * 4,
        out_specs=pl.BlockSpec(memory_space=pltpu.VMEM),
        scratch_shapes=[
            pltpu.VMEM((rows, tiles, lanes), BF16),
            pltpu.VMEM((rows, tiles, lanes), BF16),
            pltpu.VMEM((tiles, rows, lanes), BF16),
            pltpu.VMEM((tiles, rows, lanes), BF16),
            pltpu.VMEM((rows, width), F32),
            pltpu.VMEM((rows, width), F32),
            pltpu.VMEM((width, rows), F32),
            pltpu.VMEM(block, BF16),
            pltpu.VMEM(block, BF16),
            pltpu.VMEM(block, BF16),
            pltpu.VMEM(block, BF16),
            pltpu.VMEM(block, BF16),
            pltpu.VMEM(block, BF16),
            pltpu.VMEM(band_block, F32),
            pltpu.VMEM(band_block, F32),
            pltpu.VMEM(band_block, F32),
            pltpu.VMEM(band_block, F32),
            pltpu.SemaphoreType.DMA((4,)),
            pltpu.SemaphoreType.DMA((2, zc)),
            pltpu.SemaphoreType.DMA((2, zc)),
            pltpu.SemaphoreType.DMA((2, zc, group)),
            pltpu.SemaphoreType.DMA((2, zc, group)),
            pltpu.SemaphoreType.DMA((2, zc)),
            pltpu.SemaphoreType.DMA((2, zc)),
            pltpu.SemaphoreType.DMA((2, bands)),
            pltpu.SemaphoreType.DMA((2, bands)),
        ],
        compiler_params=pltpu.CompilerParams(collective_id=0, has_side_effects=True),
        name="tile_low_rank_step",
    )(ranks[0], u_factors[0], v_factors[0], observed[0], start[0])
    return jnp.transpose(result)[None]


def solution(mesh):
    in_specs = (
        P("freq", "tile", None, None),
        P("freq", "tile", None, None),
        P("freq", None, None),
        P("freq", "tile", None),
        P("freq", "tile", None),
    )
    out_specs = P("freq", "tile", None)
    return jax.shard_map(body, mesh=mesh, in_specs=in_specs, out_specs=out_specs, check_vma=False)
```

time: 128 us -> 58.1 us (0.45)
  the two profiles are of different devices: /device:TPU:1 before, /device:TPU:2 now
where the time goes in v1:
time: 58.1 us; the launch traced here: 57.9 us
  Pallas kernels  56.2 us (97%)
  local copies, waits for them, and re-layouts  1.66 us (3%)
    pallas_call x1, Pallas kernels, body(): pl.pallas_call(kernel, out_shape=jax.ShapeDtypeStruct((width, rows), F32)...  56.2 us
    broadcast_in_dim x1, local copies, waits for them, and re-layouts, body(): return jnp.transpose(result)[None]  1.66 us

profile of v1, /device:TPU:2, one launch (start us, length us, event | category | flops | bytes accessed | tf_op | source)
XLA Modules:
  0.0 57.9 jit_solution(11231660214762170217)
XLA Ops:
  0.0 56.2 %tile_low_rank_step.1 = f32[128,256]{1,0:T(8,128)} custom-call(s32[32,32]{1,0:T(8,128)} %bitcast.13, bf16[256,32,128]{2,1,0:T(8,128)(2,1)} %bitcast.8, bf16[256,32,128]{2,1,0:T(8,128)(2,1)} %bitcast.9, f32[256,128]{1,0:T(8,128)} %bitcast.11, f32[256,128]{1,0:T(8,128)} %bitcast.12), custom_call_target="tpu_custom_call" | custom-call | tf_op jit(solution)/shard_map/tile_low_rank_step/pallas_call | solution.py:338
  56.3 1.7 %copy.6 = f32[1,256,128]{2,1,0:T(8,128)} copy(f32[1,256,128]{1,2,0:T(8,128)} %bitcast.10) | data formatting | bytes 262144 | tf_op jit(solution)/shard_map/broadcast_in_dim | solution.py:374

commit v2 on v1

v2 whole, which is shorter than its diff:
```python
import contextlib
import math

import jax
import jax.numpy as jnp
from jax import lax
from jax.experimental import pallas as pl
from jax.experimental.pallas import tpu as pltpu
from jax.sharding import PartitionSpec as P

STEP_SIZE = 0.2
LEVEL = 0.5
PLANE = (8, 4)
BANDS = 8
MESH = pl.DeviceIdType.MESH
BF16 = jnp.bfloat16
F32 = jnp.float32
SPAN = 4
EDGES = (0, 5, 8)
LOADS = 4
WIRE_FORTH = BF16
WIRE_BACK = BF16


def section(name):
    return contextlib.nullcontext()


def far_first(extent):
    order = sorted(range(extent), key=lambda d: (-min(d, extent - d), d))
    return order


def twiddle_pair(real, imag, cosine, sine):
    if abs(sine) < 1e-9:
        return (real, imag) if cosine > 0 else (-real, -imag)
    if abs(cosine) < 1e-9:
        return (-imag, real) if sine > 0 else (imag, -real)
    return real * cosine - imag * sine, real * sine + imag * cosine


def small_dft(reals, imags, sign):
    count = len(reals)
    if count == 1:
        return reals, imags
    even_re, even_im = small_dft(reals[0::2], imags[0::2], sign)
    odd_re, odd_im = small_dft(reals[1::2], imags[1::2], sign)
    out_re, out_im = [None] * count, [None] * count
    half = count // 2
    for k in range(half):
        angle = sign * 2.0 * math.pi * k / count
        tr, ti = twiddle_pair(odd_re[k], odd_im[k], math.cos(angle), math.sin(angle))
        out_re[k], out_im[k] = even_re[k] + tr, even_im[k] + ti
        out_re[k + half], out_im[k + half] = even_re[k] - tr, even_im[k] - ti
    return out_re, out_im


def thin_out(values):
    return values - jnp.clip(values, -LEVEL, LEVEL)


def kernel(
    ranks_ref, u_hbm, v_hbm, observed_hbm, start_hbm, out_ref,
    u_raw, v_raw, u_tiles, v_tiles, observed_rows, start_rows, start_t, total_ref,
    pair_out, pair_own, pair_in, chip_out, chip_in, share_in,
    start_out, start_in, band_out, band_in, thin_out_buf, thin_in,
    load_sem, sent, pair_recv, chip_recv, share_recv, band_recv,
):
    zc, xc = PLANE
    group = xc // 2
    bands = BANDS
    rows = u_raw.shape[0]
    lanes = u_raw.shape[2]
    rank_half = lanes // 2
    sources2 = start_t.shape[0]
    sources = sources2 // 2
    per_band = sources // bands

    place = lax.axis_index("tile")
    band = lax.axis_index("freq")
    chip = lax.div(place, 2)
    core = lax.rem(place, 2)
    other = 1 - core
    z = lax.div(chip, xc)
    x = lax.rem(chip, xc)
    order = far_first(zc)
    span = min(SPAN, zc)
    edges = sorted({min(edge, zc) for edge in EDGES})
    steps = len(edges) - 1
    batch_of = [c for c in range(steps) for _ in range(edges[c], edges[c + 1])]
    blocks = zc * group
    self_block = order.index(0) * group

    def shift_of(m, h, owner):
        return 2 * h + lax.rem(owner + order[m], 2)

    def chip_at(m, h, owner, forward):
        dz, dx = order[m], shift_of(m, h, owner)
        if forward:
            return lax.rem(z + dz, zc) * xc + lax.rem(x + dx, xc)
        return lax.rem(z + zc - dz, zc) * xc + lax.rem(x + xc - dx, xc)

    def is_self(m, h):
        return order[m] == 0 and h == 0

    def at_tile(index):
        return {"tile": index}

    barrier = pltpu.get_barrier_semaphore()

    def hail(device):
        pl.semaphore_signal(barrier, inc=1, device_id=device, device_id_type=MESH)

    def hail_all():
        for m in range(zc):
            for h in range(group):
                target = chip_at(m, h, core, True) * 2 + core
                if is_self(m, h):
                    pl.when(core == 1)(lambda target=target: hail(at_tile(target)))
                else:
                    hail(at_tile(target))
        hail(at_tile(chip * 2 + other))
        for k in range(1, bands):
            hail({"freq": lax.rem(band + k, bands)})

    chunk = rows // LOADS

    def chunk_load(source, target, c):
        part = pl.ds(c * chunk, chunk)
        return pltpu.make_async_copy(source.at[part], target.at[part], load_sem.at[c])

    v_loads = [chunk_load(v_hbm, v_raw, c) for c in range(LOADS)]
    u_load = pltpu.make_async_copy(u_hbm, u_raw, load_sem.at[LOADS])
    start_load = pltpu.make_async_copy(start_hbm, start_rows, load_sem.at[LOADS + 1])
    observed_load = pltpu.make_async_copy(observed_hbm, observed_rows, load_sem.at[LOADS + 2])
    hail_all()
    start_load.start()
    for load in v_loads:
        load.start()
    u_load.start()
    observed_load.start()

    def retile(raw, tiles, arrivals):
        def step(b, carry):
            at = pl.multiple_of(b * 16, 16)
            tiles[:, pl.ds(at, 16), :] = jnp.swapaxes(raw[pl.ds(at, 16)], 0, 1)
            return carry

        piece = rows // 16 // len(arrivals)
        for c, load in enumerate(arrivals):
            load.wait()
            lax.fori_loop(c * piece, (c + 1) * piece, step, 0)

    lane_ids = lax.broadcasted_iota(jnp.int32, (sources, lanes), 1)
    upper = lane_ids < rank_half
    rank_ids = jnp.where(upper, lane_ids, lane_ids - rank_half)
    sign = jnp.where(upper, 1.0, -1.0).astype(F32)

    def swap_halves(values):
        return jnp.concatenate([values[:, rank_half:], values[:, :rank_half]], axis=1)

    def tile_group(tiles, m, owner, forward):
        return jnp.concatenate(
            [tiles[chip_at(m, h, owner, forward)] for h in range(group)], axis=1
        )

    def pair_copy(p, c):
        part = pl.ds(c * span * group, span * group)
        return pltpu.make_async_remote_copy(
            src_ref=pair_out.at[p, part], dst_ref=pair_in.at[p, part],
            send_sem=sent.at[0], recv_sem=pair_recv.at[p, c],
            device_id=at_tile(chip * 2 + other), device_id_type=MESH,
        )

    def chip_copy(p, m, h):
        block = m * group + h
        return pltpu.make_async_remote_copy(
            src_ref=chip_out.at[p * blocks + block], dst_ref=chip_in.at[p, block],
            send_sem=sent.at[1], recv_sem=chip_recv.at[p, batch_of[m]],
            device_id=at_tile(chip_at(m, h, core, True) * 2 + core), device_id_type=MESH,
        )

    def share_copy(p, c):
        part = pl.ds(edges[c] * group, (edges[c + 1] - edges[c]) * group)
        return pltpu.make_async_remote_copy(
            src_ref=chip_in.at[p, part], dst_ref=share_in.at[p, part],
            send_sem=sent.at[2], recv_sem=share_recv.at[p, c],
            device_id=at_tile(chip * 2 + other), device_id_type=MESH,
        )

    def arrived(target, sem):
        pltpu.make_async_remote_copy(
            src_ref=target, dst_ref=target, send_sem=sent.at[0], recv_sem=sem,
            device_id=at_tile(chip * 2 + other), device_id_type=MESH,
        ).wait_recv()

    def departed(source, sem):
        pltpu.make_async_remote_copy(
            src_ref=source, dst_ref=source, send_sem=sem, recv_sem=band_recv.at[0],
            device_id=at_tile(chip * 2 + other), device_id_type=MESH,
        ).wait_send()

    def chips_arrived(p, c):
        first, count = edges[c] * group, (edges[c + 1] - edges[c]) * group
        sem = chip_recv.at[p, c]
        if first <= self_block < first + count:
            @pl.when(core == 0)
            def _():
                if count > 1:
                    arrived(chip_in.at[p, pl.ds(first, count - 1)], sem)

            @pl.when(core == 1)
            def _():
                arrived(chip_in.at[p, pl.ds(first, count)], sem)
        else:
            arrived(chip_in.at[p, pl.ds(first, count)], sem)

    def remote_only(m, h, act):
        if is_self(m, h):
            pl.when(core == 1)(act)
        else:
            act()

    def project(left, tiles, m, owner):
        product = jnp.dot(
            left, tile_group(tiles, m, owner, True), preferred_element_type=F32
        )
        parts = []
        for h in range(group):
            block = product[:, h * lanes : (h + 1) * lanes]
            parts.append(
                (block[:sources] * sign + swap_halves(block[sources:])).astype(BF16)
            )
        return parts

    chunks = range(zc // span)

    def scatter(p, left, tiles, rank_of, ready):
        def fill(target, owner, c):
            for m in range(c * span, (c + 1) * span):
                for h, part in enumerate(project(left, tiles, m, owner)):
                    target[p, m * group + h] = part

        def finish(m):
            for h in range(group):
                block = m * group + h
                total = pair_own[p, block].astype(F32) + pair_in[p, block].astype(F32)
                rank = rank_of(chip_at(m, h, core, True))
                total = jnp.where(rank_ids < rank, total, 0.0).astype(BF16)
                chip_out[p * blocks + block] = total
                if is_self(m, h):
                    @pl.when(core == 0)
                    def _(total=total, block=block):
                        chip_in[p, block] = total

        with section("give%d" % p):
            for c in chunks:
                fill(pair_out, other, c)
                if ready is None:
                    pair_copy(p, c).start()
        if ready is not None:
            with section("keep%d" % p):
                for c in chunks:
                    fill(pair_own, core, c)
            with section("ready"):
                ready()
            for c in chunks:
                pair_copy(p, c).start()
        for c in chunks:
            if ready is None:
                with section("keep%d_%d" % (p, c)):
                    fill(pair_own, core, c)
            with section("pairwait%d_%d" % (p, c)):
                pair_copy(p, c).wait_recv()
            with section("finish%d_%d" % (p, c)):
                for m in range(c * span, (c + 1) * span):
                    finish(m)
                    for h in range(group):
                        remote_only(m, h, lambda m=m, h=h: chip_copy(p, m, h).start())

    def stacked(coeffs):
        wide = coeffs.astype(F32)
        return jnp.concatenate([wide * sign, swap_halves(wide)], axis=0).astype(BF16)

    def expand(block, tiles, m, owner):
        left = jnp.concatenate([stacked(part) for part in block], axis=1)
        right = tile_group(tiles, m, owner, False)
        return lax.dot_general(
            left, right, (((1,), (1,)), ((), ())), preferred_element_type=F32
        )

    def collect(p, tiles):
        def terms(source, c, owner):
            total = None
            for m in range(edges[c], edges[c + 1]):
                block = [source[p, m * group + h] for h in range(group)]
                term = expand(block, tiles, m, owner)
                total = term if total is None else total + term
            return total

        for c in range(steps + 1):
            if c < steps:
                with section("chipwait%d_%d" % (p, c)):
                    chips_arrived(p, c)
                share_copy(p, c).start()
                with section("expand%d_%d" % (p, c)):
                    term = terms(chip_in, c, core)
                    total_ref[...] = term if c == 0 else total_ref[...] + term
            if c > 0:
                with section("sharewait%d_%d" % (p, c - 1)):
                    share_copy(p, c - 1).wait_recv()
                with section("shared%d_%d" % (p, c - 1)):
                    term = total_ref[...] + terms(share_in, c - 1, other)
                    if c < steps:
                        total_ref[...] = term
        return term

    wires = ((band_out, band_in), (thin_out_buf, thin_in), (start_out, start_in))

    def band_copy(p, k):
        target = lax.rem(band + k, bands)
        src, dst = wires[p]
        return pltpu.make_async_remote_copy(
            src_ref=src.at[target], dst_ref=dst.at[band],
            send_sem=sent.at[3 + p], recv_sem=band_recv.at[p],
            device_id={"freq": target}, device_id_type=MESH,
        )

    band_order = [k for k in far_first(bands) if k > 0]

    def to_slabs(values, target):
        for q in range(bands):
            low = q * per_band
            slab = jnp.concatenate(
                [values[low : low + per_band], values[sources + low : sources + low + per_band]],
                axis=0,
            )
            target[q] = slab.astype(target.dtype)

    with section("start"):
        start_load.wait()
        start_t[...] = jnp.transpose(start_rows[...])
        to_slabs(start_t[...], start_out)
        start_in[band] = start_out[band]
    with section("retile_v"):
        retile(v_raw, v_tiles, v_loads)
    scatter(
        0, start_t[...].astype(BF16), v_tiles,
        lambda target: ranks_ref[target, chip],
        lambda: pl.semaphore_wait(barrier, zc * group + bands - 1 + core),
    )
    for k in band_order:
        band_copy(2, k).start()
    with section("retile_u"):
        retile(u_raw, u_tiles, [u_load])
        observed_load.wait()
        observed_t = jnp.transpose(observed_rows[...])
    misfit = collect(0, u_tiles) - observed_t
    scatter(
        1, misfit.astype(BF16), u_tiles,
        lambda target: ranks_ref[chip, target],
        None,
    )
    change = -STEP_SIZE * collect(1, v_tiles)

    to_slabs(change, band_out)
    for k in band_order:
        band_copy(0, k).start()
    band_in[band] = band_out[band]
    with section("bandwait0"):
        arrived(start_in.at[pl.ds(0, bands - 1)], band_recv.at[2])
        arrived(band_in.at[pl.ds(0, bands - 1)], band_recv.at[0])

    scale = 1.0 / math.sqrt(bands)
    slabs = [start_in[f] + band_in[f].astype(F32) for f in range(bands)]
    reals = [slab[:per_band] for slab in slabs]
    imags = [slab[per_band:] for slab in slabs]
    reals, imags = small_dft(reals, imags, 1.0)
    reals = [thin_out(value * scale) for value in reals]
    imags = [thin_out(value * scale) for value in imags]
    reals, imags = small_dft(reals, imags, -1.0)
    for f in range(bands):
        slab = jnp.concatenate([reals[f], imags[f]], axis=0) * scale
        thin_out_buf[f] = slab.astype(thin_out_buf.dtype)
    for k in band_order:
        band_copy(1, k).start()
    thin_in[band] = thin_out_buf[band]
    with section("bandwait1"):
        arrived(thin_in.at[pl.ds(0, bands - 1)], band_recv.at[1])
    with section("out"):
        slabs = [thin_in[q].astype(F32) for q in range(bands)]
        whole = jnp.concatenate(
            [slab[:per_band] for slab in slabs] + [slab[per_band:] for slab in slabs], axis=0
        )
        out_ref[...] = jnp.transpose(whole)

    with section("tail"):
        departed(pair_out, sent.at[0])
        departed(chip_in, sent.at[2])
        for p in range(3):
            departed(wires[p][0].at[pl.ds(0, bands - 1)], sent.at[3 + p])

        @pl.when(core == 0)
        def _():
            departed(chip_out.at[pl.ds(0, 2 * blocks - 2)], sent.at[1])

        @pl.when(core == 1)
        def _():
            departed(chip_out, sent.at[1])


def body(u_factors, v_factors, ranks, observed, start):
    zc, xc = PLANE
    bands = BANDS
    _, rows, tiles, lanes = u_factors.shape
    width = start.shape[2]
    group = xc // 2
    sources = width // 2
    per_band = sources // bands
    any_spec = pl.BlockSpec(memory_space=pl.ANY)
    block = (2, zc * group, sources, lanes)
    band_block = (bands, 2 * per_band, rows)
    result = pl.pallas_call(
        kernel,
        out_shape=pltpu.MemorySpace.VMEM((rows, width), F32),
        in_specs=[pl.BlockSpec(memory_space=pltpu.SMEM)] + [any_spec] * 4,
        out_specs=pl.BlockSpec(memory_space=pltpu.VMEM),
        scratch_shapes=[
            pltpu.VMEM((rows, tiles, lanes), BF16),
            pltpu.VMEM((rows, tiles, lanes), BF16),
            pltpu.VMEM((tiles, rows, lanes), BF16),
            pltpu.VMEM((tiles, rows, lanes), BF16),
            pltpu.VMEM((rows, width), F32),
            pltpu.VMEM((rows, width), F32),
            pltpu.VMEM((width, rows), F32),
            pltpu.VMEM((width, rows), F32),
            pltpu.VMEM(block, BF16),
            pltpu.VMEM(block, BF16),
            pltpu.VMEM(block, BF16),
            pltpu.VMEM((2 * zc * group, sources, lanes), BF16),
            pltpu.VMEM(block, BF16),
            pltpu.VMEM(block, BF16),
            pltpu.VMEM(band_block, F32),
            pltpu.VMEM(band_block, F32),
            pltpu.VMEM(band_block, WIRE_FORTH),
            pltpu.VMEM(band_block, WIRE_FORTH),
            pltpu.VMEM(band_block, WIRE_BACK),
            pltpu.VMEM(band_block, WIRE_BACK),
            pltpu.SemaphoreType.DMA((LOADS + 3,)),
            pltpu.SemaphoreType.DMA((6,)),
            pltpu.SemaphoreType.DMA((2, max(zc // SPAN, 1))),
            pltpu.SemaphoreType.DMA((2, len(EDGES))),
            pltpu.SemaphoreType.DMA((2, len(EDGES))),
            pltpu.SemaphoreType.DMA((3,)),
        ],
        compiler_params=pltpu.CompilerParams(collective_id=0, has_side_effects=True),
        name="tile_low_rank_step",
    )(ranks[0], u_factors[0], v_factors[0], observed[0], start[0])
    return result[None]


def solution(mesh):
    in_specs = (
        P("freq", "tile", None, None),
        P("freq", "tile", None, None),
        P("freq", None, None),
        P("freq", "tile", None),
        P("freq", "tile", None),
    )
    out_specs = P("freq", "tile", None)
    return jax.shard_map(body, mesh=mesh, in_specs=in_specs, out_specs=out_specs, check_vma=False)
```

time: 58.1 us -> 49.9 us (0.86)
  the two profiles are of different devices: /device:TPU:2 before, /device:TPU:1 now
where the time goes in v2:
time: 49.9 us; the launch traced here: 49.7 us
  Pallas kernels  49.1 us (98%)
  local copies, waits for them, and re-layouts  0.66 us (1%)
    pallas_call x1, Pallas kernels, body(): pl.pallas_call(kernel, out_shape=pltpu.MemorySpace.VMEM((rows, width), F3...  49.1 us

profile of v2, /device:TPU:1, one launch (start us, length us, event | category | flops | bytes accessed | tf_op | source)
XLA Modules:
  0.0 49.7 jit_solution(15614477160987265644)
XLA Ops:
  0.0 49.1 %tile_low_rank_step.1 = f32[256,128]{1,0:T(8,128)S(1)} custom-call(s32[32,32]{1,0:T(8,128)} %bitcast.11, bf16[256,32,128]{2,1,0:T(8,128)(2,1)} %bitcast.7, bf16[256,32,128]{2,1,0:T(8,128)(2,1)} %bitcast.8, f32[256,128]{1,0:T(8,128)} %bitcast.9, f32[256,128]{1,0:T(8,128)} %bitcast.10), custom_call_target="tpu_custom_call" | custom-call | tf_op jit(solution)/shard_map/tile_low_rank_step/pallas_call | solution.py:423
  49.1 0.7 %copy.7 = f32[1,256,128]{2,1,0:T(8,128)} copy(f32[1,256,128]{2,1,0:T(8,128)S(1)} %bitcast.6) | data formatting | bytes 262144

commit v3 on v2

--- a/solution.py
+++ b/solution.py
@@ -16,7 +16,8 @@
 BF16 = jnp.bfloat16
 F32 = jnp.float32
 SPAN = 4
-EDGES = (0, 5, 8)
+STRIDE = 4
+EDGES = (0, 4, 8)
 LOADS = 4
 WIRE_FORTH = BF16
 WIRE_BACK = BF16
@@ -62,9 +63,10 @@
 def kernel(
     ranks_ref, u_hbm, v_hbm, observed_hbm, start_hbm, out_ref,
     u_raw, v_raw, u_tiles, v_tiles, observed_rows, start_rows, start_t, total_ref,
+    u_far, image_out, image_in,
     pair_out, pair_own, pair_in, chip_out, chip_in, share_in,
     start_out, start_in, band_out, band_in, thin_out_buf, thin_in,
-    load_sem, sent, pair_recv, chip_recv, share_recv, band_recv,
+    load_sem, sent, pair_recv, chip_recv, share_recv, band_recv, far_recv, image_recv,
 ):
     zc, xc = PLANE
     group = xc // 2
@@ -84,7 +86,7 @@
     z = lax.div(chip, xc)
     x = lax.rem(chip, xc)
     order = far_first(zc)
-    span = min(SPAN, zc)
+    span, stride = min(SPAN, zc), min(STRIDE, zc)
     edges = sorted({min(edge, zc) for edge in EDGES})
     steps = len(edges) - 1
     batch_of = [c for c in range(steps) for _ in range(edges[c], edges[c + 1])]
@@ -164,11 +166,16 @@
             [tiles[chip_at(m, h, owner, forward)] for h in range(group)], axis=1
         )
 
-    def pair_copy(p, c):
+    def far_group(m, forward):
+        return jnp.concatenate(
+            [u_far[lax.div(chip_at(m, h, core, forward), 2)] for h in range(group)], axis=1
+        )
+
+    def pair_copy(c):
         part = pl.ds(c * span * group, span * group)
         return pltpu.make_async_remote_copy(
-            src_ref=pair_out.at[p, part], dst_ref=pair_in.at[p, part],
-            send_sem=sent.at[0], recv_sem=pair_recv.at[p, c],
+            src_ref=pair_out.at[part], dst_ref=pair_in.at[part],
+            send_sem=sent.at[0], recv_sem=pair_recv.at[c],
             device_id=at_tile(chip * 2 + other), device_id_type=MESH,
         )
 
@@ -180,11 +187,26 @@
             device_id=at_tile(chip_at(m, h, core, True) * 2 + core), device_id_type=MESH,
         )
 
-    def share_copy(p, c):
+    def share_copy(c):
         part = pl.ds(edges[c] * group, (edges[c + 1] - edges[c]) * group)
         return pltpu.make_async_remote_copy(
-            src_ref=chip_in.at[p, part], dst_ref=share_in.at[p, part],
-            send_sem=sent.at[2], recv_sem=share_recv.at[p, c],
+            src_ref=chip_in.at[1, part], dst_ref=share_in.at[part],
+            send_sem=sent.at[2], recv_sem=share_recv.at[c],
+            device_id=at_tile(chip * 2 + other), device_id_type=MESH,
+        )
+
+    def far_copy(m, h):
+        tile = chip_at(m, h, other, True)
+        return pltpu.make_async_remote_copy(
+            src_ref=u_tiles.at[tile], dst_ref=u_far.at[lax.div(tile, 2)],
+            send_sem=sent.at[6], recv_sem=far_recv.at[0],
+            device_id=at_tile(chip * 2 + other), device_id_type=MESH,
+        )
+
+    def image_copy(half):
+        return pltpu.make_async_remote_copy(
+            src_ref=image_out.at[half], dst_ref=image_in.at[1 - half],
+            send_sem=sent.at[7], recv_sem=image_recv.at[1 - half],
             device_id=at_tile(chip * 2 + other), device_id_type=MESH,
         )
 
@@ -221,95 +243,128 @@
         else:
             act()
 
-    def project(left, tiles, m, owner):
-        product = jnp.dot(
-            left, tile_group(tiles, m, owner, True), preferred_element_type=F32
-        )
+    def project(left, right):
+        product = jnp.dot(left, right, preferred_element_type=F32)
         parts = []
         for h in range(group):
             block = product[:, h * lanes : (h + 1) * lanes]
-            parts.append(
-                (block[:sources] * sign + swap_halves(block[sources:])).astype(BF16)
-            )
+            parts.append(block[:sources] * sign + swap_halves(block[sources:]))
         return parts
 
+    def masked(part, rank):
+        return jnp.where(rank_ids < rank, part, 0.0).astype(BF16)
+
+    def post(p, m, parts):
+        for h, part in enumerate(parts):
+            block = m * group + h
+            chip_out[p * blocks + block] = part
+            if is_self(m, h):
+                @pl.when(core == 0)
+                def _(part=part, block=block):
+                    chip_in[p, block] = part
+
+        for h in range(group):
+            remote_only(m, h, lambda m=m, h=h: chip_copy(p, m, h).start())
+
     chunks = range(zc // span)
 
-    def scatter(p, left, tiles, rank_of, ready):
-        def fill(target, owner, c):
-            for m in range(c * span, (c + 1) * span):
-                for h, part in enumerate(project(left, tiles, m, owner)):
-                    target[p, m * group + h] = part
-
-        def finish(m):
-            for h in range(group):
-                block = m * group + h
-                total = pair_own[p, block].astype(F32) + pair_in[p, block].astype(F32)
-                rank = rank_of(chip_at(m, h, core, True))
-                total = jnp.where(rank_ids < rank, total, 0.0).astype(BF16)
-                chip_out[p * blocks + block] = total
-                if is_self(m, h):
-                    @pl.when(core == 0)
-                    def _(total=total, block=block):
-                        chip_in[p, block] = total
-
-        with section("give%d" % p):
-            for c in chunks:
-                fill(pair_out, other, c)
-                if ready is None:
-                    pair_copy(p, c).start()
-        if ready is not None:
-            with section("keep%d" % p):
-                for c in chunks:
-                    fill(pair_own, core, c)
-            with section("ready"):
-                ready()
-            for c in chunks:
-                pair_copy(p, c).start()
+    def scatter_first(left, ready):
+        def fill(target, owner):
+            for m in range(zc):
+                for h, part in enumerate(project(left, tile_group(v_tiles, m, owner, True))):
+                    target[m * group + h] = part.astype(BF16)
+
+        with section("give0"):
+            fill(pair_out, other)
+        with section("keep0"):
+            fill(pair_own, core)
+        with section("ready"):
+            ready()
         for c in chunks:
-            if ready is None:
-                with section("keep%d_%d" % (p, c)):
-                    fill(pair_own, core, c)
-            with section("pairwait%d_%d" % (p, c)):
-                pair_copy(p, c).wait_recv()
-            with section("finish%d_%d" % (p, c)):
+            pair_copy(c).start()
+        for c in chunks:
+            with section("pairwait0_%d" % c):
+                pair_copy(c).wait_recv()
+            with section("finish0_%d" % c):
                 for m in range(c * span, (c + 1) * span):
-                    finish(m)
+                    parts = []
                     for h in range(group):
-                        remote_only(m, h, lambda m=m, h=h: chip_copy(p, m, h).start())
+                        block = m * group + h
+                        total = pair_own[block].astype(F32) + pair_in[block].astype(F32)
+                        parts.append(masked(total, ranks_ref[chip_at(m, h, core, True), chip]))
+                    post(0, m, parts)
+
+    def scatter_second(left):
+        for c in range(zc // stride):
+            with section("project1_%d" % c):
+                ready = []
+                for m in range(c * stride, (c + 1) * stride):
+                    right = jnp.concatenate(
+                        [tile_group(u_tiles, m, core, True), far_group(m, True)], axis=0
+                    )
+                    ready.append([
+                        masked(part, ranks_ref[chip, chip_at(m, h, core, True)])
+                        for h, part in enumerate(project(left, right))
+                    ])
+                for i, parts in enumerate(ready):
+                    post(1, c * stride + i, parts)
 
     def stacked(coeffs):
         wide = coeffs.astype(F32)
         return jnp.concatenate([wide * sign, swap_halves(wide)], axis=0).astype(BF16)
 
-    def expand(block, tiles, m, owner):
-        left = jnp.concatenate([stacked(part) for part in block], axis=1)
-        right = tile_group(tiles, m, owner, False)
+    def expand(left, right):
         return lax.dot_general(
             left, right, (((1,), (1,)), ((), ())), preferred_element_type=F32
         )
 
-    def collect(p, tiles):
+    def gathered(block):
+        return jnp.concatenate([stacked(part) for part in block], axis=1)
+
+    def collect_first():
+        for c in range(steps):
+            with section("chipwait0_%d" % c):
+                chips_arrived(0, c)
+                if c == 0:
+                    arrived(u_far, far_recv.at[0])
+            with section("expand0_%d" % c):
+                members = range(edges[c], edges[c + 1])
+                lefts = [gathered([chip_in[0, m * group + h] for h in range(group)]) for m in members]
+                for half in (1, 0):
+                    total = None if c == 0 and half else image_out[half]
+                    for m, left in zip(members, lefts):
+                        right = far_group(m, False) if half else tile_group(u_tiles, m, core, False)
+                        term = expand(left, right)
+                        total = term if total is None else total + term
+                    image_out[half] = total
+                    if c == steps - 1:
+                        image_copy(half).start()
+        with section("imagewait"):
+            for half in (0, 1):
+                image_copy(1 - half).wait_recv()
+        return jnp.concatenate([image_out[half] + image_in[half] for half in (0, 1)], axis=1)
+
+    def collect_second():
         def terms(source, c, owner):
             total = None
             for m in range(edges[c], edges[c + 1]):
-                block = [source[p, m * group + h] for h in range(group)]
-                term = expand(block, tiles, m, owner)
+                left = gathered([source[m * group + h] for h in range(group)])
+                term = expand(left, tile_group(v_tiles, m, owner, False))
                 total = term if total is None else total + term
             return total
 
         for c in range(steps + 1):
             if c < steps:
-                with section("chipwait%d_%d" % (p, c)):
-                    chips_arrived(p, c)
-                share_copy(p, c).start()
-                with section("expand%d_%d" % (p, c)):
-                    term = terms(chip_in, c, core)
+                with section("chipwait1_%d" % c):
+                    chips_arrived(1, c)
+                share_copy(c).start()
+                with section("expand1_%d" % c):
+                    term = terms(chip_in.at[1], c, core)
                     total_ref[...] = term if c == 0 else total_ref[...] + term
             if c > 0:
-                with section("sharewait%d_%d" % (p, c - 1)):
-                    share_copy(p, c - 1).wait_recv()
-                with section("shared%d_%d" % (p, c - 1)):
+                with section("sharewait1_%d" % (c - 1)):
+                    share_copy(c - 1).wait_recv()
+                with section("shared1_%d" % (c - 1)):
                     term = total_ref[...] + terms(share_in, c - 1, other)
                     if c < steps:
                         total_ref[...] = term
@@ -344,24 +399,22 @@
         start_in[band] = start_out[band]
     with section("retile_v"):
         retile(v_raw, v_tiles, v_loads)
-    scatter(
-        0, start_t[...].astype(BF16), v_tiles,
-        lambda target: ranks_ref[target, chip],
+    scatter_first(
+        start_t[...].astype(BF16),
         lambda: pl.semaphore_wait(barrier, zc * group + bands - 1 + core),
     )
-    for k in band_order:
-        band_copy(2, k).start()
     with section("retile_u"):
         retile(u_raw, u_tiles, [u_load])
+        for m in range(zc):
+            for h in range(group):
+                far_copy(m, h).start()
+        for k in band_order:
+            band_copy(2, k).start()
         observed_load.wait()
-        observed_t = jnp.transpose(observed_rows[...])
-    misfit = collect(0, u_tiles) - observed_t
-    scatter(
-        1, misfit.astype(BF16), u_tiles,
-        lambda target: ranks_ref[chip, target],
-        None,
-    )
-    change = -STEP_SIZE * collect(1, v_tiles)
+        image_out[0] = -jnp.transpose(observed_rows[...])
+    misfit = collect_first()
+    scatter_second(misfit.astype(BF16))
+    change = -STEP_SIZE * collect_second()
 
     to_slabs(change, band_out)
     for k in band_order:
@@ -396,7 +449,9 @@
 
     with section("tail"):
         departed(pair_out, sent.at[0])
-        departed(chip_in, sent.at[2])
+        departed(chip_in.at[1], sent.at[2])
+        departed(u_far, sent.at[6])
+        departed(image_out, sent.at[7])
         for p in range(3):
             departed(wires[p][0].at[pl.ds(0, bands - 1)], sent.at[3 + p])
 
@@ -418,7 +473,7 @@
     sources = width // 2
     per_band = sources // bands
     any_spec = pl.BlockSpec(memory_space=pl.ANY)
-    block = (2, zc * group, sources, lanes)
+    block = (zc * group, sources, lanes)
     band_block = (bands, 2 * per_band, rows)
     result = pl.pallas_call(
         kernel,
@@ -434,11 +489,14 @@
             pltpu.VMEM((rows, width), F32),
             pltpu.VMEM((width, rows), F32),
             pltpu.VMEM((width, rows), F32),
+            pltpu.VMEM((tiles // 2, rows, lanes), BF16),
+            pltpu.VMEM((2, width, rows), F32),
+            pltpu.VMEM((2, width, rows), F32),
             pltpu.VMEM(block, BF16),
             pltpu.VMEM(block, BF16),
             pltpu.VMEM(block, BF16),
             pltpu.VMEM((2 * zc * group, sources, lanes), BF16),
-            pltpu.VMEM(block, BF16),
+            pltpu.VMEM((2,) + block, BF16),
             pltpu.VMEM(block, BF16),
             pltpu.VMEM(band_block, F32),
             pltpu.VMEM(band_block, F32),
@@ -447,11 +505,13 @@
             pltpu.VMEM(band_block, WIRE_BACK),
             pltpu.VMEM(band_block, WIRE_BACK),
             pltpu.SemaphoreType.DMA((LOADS + 3,)),
-            pltpu.SemaphoreType.DMA((6,)),
-            pltpu.SemaphoreType.DMA((2, max(zc // SPAN, 1))),
+            pltpu.SemaphoreType.DMA((8,)),
+            pltpu.SemaphoreType.DMA((max(zc // SPAN, 1),)),
             pltpu.SemaphoreType.DMA((2, len(EDGES))),
-            pltpu.SemaphoreType.DMA((2, len(EDGES))),
+            pltpu.SemaphoreType.DMA((len(EDGES),)),
             pltpu.SemaphoreType.DMA((3,)),
+            pltpu.SemaphoreType.DMA((1,)),
+            pltpu.SemaphoreType.DMA((2,)),
         ],
         compiler_params=pltpu.CompilerParams(collective_id=0, has_side_effects=True),
         name="tile_low_rank_step",

time: 49.9 us -> 48.9 us (0.980)
  Pallas kernels: 49.1 us -> 48.1 us
    pallas_call x1, Pallas kernels: 49.1 us -> 48.1 us  [body(): pl.pallas_call(kernel, out_shape=pltpu.MemorySpace.VMEM((rows, width), F3...]
where the time goes in v3:
time: 48.9 us; the launch traced here: 48.7 us
  Pallas kernels  48.1 us (98%)
  local copies, waits for them, and re-layouts  0.66 us (1%)
    pallas_call x1, Pallas kernels, body(): pl.pallas_call(kernel, out_shape=pltpu.MemorySpace.VMEM((rows, width), F3...  48.1 us

profile of v3, /device:TPU:1, one launch (start us, length us, event | category | flops | bytes accessed | tf_op | source)
XLA Modules:
  0.0 48.7 jit_solution(10525259521673984163)
XLA Ops:
  0.0 48.1 %tile_low_rank_step.1 = f32[256,128]{1,0:T(8,128)S(1)} custom-call(s32[32,32]{1,0:T(8,128)} %bitcast.11, bf16[256,32,128]{2,1,0:T(8,128)(2,1)} %bitcast.7, bf16[256,32,128]{2,1,0:T(8,128)(2,1)} %bitcast.8, f32[256,128]{1,0:T(8,128)} %bitcast.9, f32[256,128]{1,0:T(8,128)} %bitcast.10), custom_call_target="tpu_custom_call" | custom-call | tf_op jit(solution)/shard_map/tile_low_rank_step/pallas_call | solution.py:478
  48.1 0.7 %copy.7 = f32[1,256,128]{2,1,0:T(8,128)} copy(f32[1,256,128]{2,1,0:T(8,128)S(1)} %bitcast.6) | data formatting | bytes 262144

commit v4 on v3

--- a/solution.py
+++ b/solution.py
@@ -61,8 +61,8 @@
 
 
 def kernel(
-    ranks_ref, u_hbm, v_hbm, observed_hbm, start_hbm, out_ref,
-    u_raw, v_raw, u_tiles, v_tiles, observed_rows, start_rows, start_t, total_ref,
+    ranks_hbm, u_hbm, v_hbm, observed_hbm, start_hbm, out_ref,
+    ranks_ref, u_raw, v_raw, u_tiles, v_tiles, observed_rows, start_rows, start_t, total_ref,
     u_far, image_out, image_in,
     pair_out, pair_own, pair_in, chip_out, chip_in, share_in,
     start_out, start_in, band_out, band_in, thin_out_buf, thin_in,
@@ -136,9 +136,11 @@
     start_load = pltpu.make_async_copy(start_hbm, start_rows, load_sem.at[LOADS + 1])
     observed_load = pltpu.make_async_copy(observed_hbm, observed_rows, load_sem.at[LOADS + 2])
     hail_all()
+    ranks_load = pltpu.make_async_copy(ranks_hbm, ranks_ref, load_sem.at[LOADS + 3])
     start_load.start()
     for load in v_loads:
         load.start()
+    ranks_load.start()
     u_load.start()
     observed_load.start()
 
@@ -278,6 +280,7 @@
             fill(pair_out, other)
         with section("keep0"):
             fill(pair_own, core)
+            ranks_load.wait()
         with section("ready"):
             ready()
         for c in chunks:
@@ -478,9 +481,10 @@
     result = pl.pallas_call(
         kernel,
         out_shape=pltpu.MemorySpace.VMEM((rows, width), F32),
-        in_specs=[pl.BlockSpec(memory_space=pltpu.SMEM)] + [any_spec] * 4,
+        in_specs=[any_spec] * 5,
         out_specs=pl.BlockSpec(memory_space=pltpu.VMEM),
         scratch_shapes=[
+            pltpu.SMEM(ranks.shape[1:], jnp.int32),
             pltpu.VMEM((rows, tiles, lanes), BF16),
             pltpu.VMEM((rows, tiles, lanes), BF16),
             pltpu.VMEM((tiles, rows, lanes), BF16),
@@ -504,7 +508,7 @@
             pltpu.VMEM(band_block, WIRE_FORTH),
             pltpu.VMEM(band_block, WIRE_BACK),
             pltpu.VMEM(band_block, WIRE_BACK),
-            pltpu.SemaphoreType.DMA((LOADS + 3,)),
+            pltpu.SemaphoreType.DMA((LOADS + 4,)),
             pltpu.SemaphoreType.DMA((8,)),
             pltpu.SemaphoreType.DMA((max(zc // SPAN, 1),)),
             pltpu.SemaphoreType.DMA((2, len(EDGES))),

time: 48.9 us -> 47.9 us (0.980)
  Pallas kernels: 48.1 us -> 47.1 us
    pallas_call x1, Pallas kernels: 48.1 us -> 47.1 us  [body(): pl.pallas_call(kernel, out_shape=pltpu.MemorySpace.VMEM((rows, width), F3...]
where the time goes in v4:
time: 47.9 us; the launch traced here: 47.8 us
  Pallas kernels  47.1 us (98%)
  local copies, waits for them, and re-layouts  0.66 us (1%)
    pallas_call x1, Pallas kernels, body(): pl.pallas_call(kernel, out_shape=pltpu.MemorySpace.VMEM((rows, width), F3...  47.1 us

profile of v4, /device:TPU:1, one launch (start us, length us, event | category | flops | bytes accessed | tf_op | source)
XLA Modules:
  0.0 47.8 jit_solution(16694533855249045044)
XLA Ops:
  0.0 47.1 %tile_low_rank_step.1 = f32[256,128]{1,0:T(8,128)S(1)} custom-call(s32[32,32]{1,0:T(8,128)} %bitcast.11, bf16[256,32,128]{2,1,0:T(8,128)(2,1)} %bitcast.7, bf16[256,32,128]{2,1,0:T(8,128)(2,1)} %bitcast.8, f32[256,128]{1,0:T(8,128)} %bitcast.9, f32[256,128]{1,0:T(8,128)} %bitcast.10), custom_call_target="tpu_custom_call" | custom-call | tf_op jit(solution)/shard_map/tile_low_rank_step/pallas_call | solution.py:481
  47.1 0.7 %copy.7 = f32[1,256,128]{2,1,0:T(8,128)} copy(f32[1,256,128]{2,1,0:T(8,128)S(1)} %bitcast.6) | data formatting | bytes 262144

commit v5 on v4

--- a/solution.py
+++ b/solution.py
@@ -265,7 +265,7 @@
                 def _(part=part, block=block):
                     chip_in[p, block] = part
 
-        for h in range(group):
+        for h in (reversed(range(group)) if p == 0 else range(group)):
             remote_only(m, h, lambda m=m, h=h: chip_copy(p, m, h).start())
 
     chunks = range(zc // span)

time: 47.9 us -> 47.4 us (0.990)
  Pallas kernels: 47.1 us -> 46.6 us
    pallas_call x1, Pallas kernels: 47.1 us -> 46.6 us  [body(): pl.pallas_call(kernel, out_shape=pltpu.MemorySpace.VMEM((rows, width), F3...]
where the time goes in v5:
time: 47.4 us; the launch traced here: 47.3 us
  Pallas kernels  46.6 us (98%)
  local copies, waits for them, and re-layouts  0.66 us (1%)
    pallas_call x1, Pallas kernels, body(): pl.pallas_call(kernel, out_shape=pltpu.MemorySpace.VMEM((rows, width), F3...  46.6 us

profile of v5, /device:TPU:1, one launch (start us, length us, event | category | flops | bytes accessed | tf_op | source)
XLA Modules:
  0.0 47.3 jit_solution(1503909719610906961)
XLA Ops:
  0.0 46.6 %tile_low_rank_step.1 = f32[256,128]{1,0:T(8,128)S(1)} custom-call(s32[32,32]{1,0:T(8,128)} %bitcast.11, bf16[256,32,128]{2,1,0:T(8,128)(2,1)} %bitcast.7, bf16[256,32,128]{2,1,0:T(8,128)(2,1)} %bitcast.8, f32[256,128]{1,0:T(8,128)} %bitcast.9, f32[256,128]{1,0:T(8,128)} %bitcast.10), custom_call_target="tpu_custom_call" | custom-call | tf_op jit(solution)/shard_map/tile_low_rank_step/pallas_call | solution.py:481
  46.6 0.7 %copy.7 = f32[1,256,128]{2,1,0:T(8,128)} copy(f32[1,256,128]{2,1,0:T(8,128)S(1)} %bitcast.6) | data formatting | bytes 262144
